TPU v7x, 128 devices: a whole 4x4x4 slice. The times are simulated.
128 devices in a mesh: gx: 16 (over z, y_hi, core), gy: 8 (over y_lo, x).
Axes of the slice: x: 4, y: 4 (y_hi: 2, y_lo: 2; y = y_hi * 2 + y_lo), z: 4, core: 2. Of those that a mesh axis runs over, the one named last changes fastest.
Arguments:
- features: bfloat16 [16, 8, 32, 64, 256], P('gx', 'gy'), may hold values from -6 to 6
- weights: bfloat16 [27, 256, 256], replicated, may hold values from -0.078125 to 0.078125
- cotangent: bfloat16 [16, 8, 32, 64, 256], P('gx', 'gy'), may hold values from -6 to 6
- send_lists: int32 [16, 8, 8, 8], P('gx', 'gy'), may hold values from 0 to 31, as said below
- block_offset: int32 [16, 8, 108], P('gx', 'gy'), may hold values from 0 to 26, as said below
- block_input: int32 [16, 8, 108, 8], P('gx', 'gy'), may hold values from 0 to 95
- block_output: int32 [16, 8, 108, 8], P('gx', 'gy'), may hold values from 0 to 32, as said below
- block_count: int32 [16, 8], P('gx', 'gy'), may hold values from 1 to 108, as said below
Outputs:
- out_features: bfloat16 [16, 8, 32, 64, 256], P('gx', 'gy')
- feat_grad: bfloat16 [16, 8, 32, 64, 256], P('gx', 'gy')
- weight_grad: float32 [27, 256, 256], replicated
Inputs may be any that keep to these rules, and one draw needn't show every extreme that they name: `send_lists`: each of a device's 8 lists names 8 different tiles that the device holds. `block_offset`: 0 in blocks past block_count. `block_output`: 32 marks an unused pair; a device's used pairs of one offset name different tiles; the used blocks come first, grouped by offset, and blocks past block_count hold only unused pairs. `block_count`: some device uses all 108 blocks.
All inputs are finite; a program needn't handle non-finite values.
Results may differ from a plain program's by a relative error of at most 0.0029.
Values may be sent and summed in bfloat16 or wider, within the bound.
A program may use at most 128 MiB of HBM per device.

v0:
```python
import math
import jax
import jax.numpy as jnp
from jax import lax
from jax.sharding import PartitionSpec as P

DIRECTIONS = ((-1, -1), (-1, 0), (-1, 1), (0, -1), (0, 1), (1, -1), (1, 0), (1, 1))


def passed_along(x, axis, by):
    size = lax.axis_size(axis)
    pairs = [(i, i + by) for i in range(size) if 0 <= i + by < size]
    return lax.ppermute(x, axis, pairs)


def travel(packet, step_x, step_y):
    moved = packet
    if step_x != 0:
        moved = passed_along(moved, "gx", step_x)
    if step_y != 0:
        moved = passed_along(moved, "gy", step_y)
    return moved


def travel_back(packet, step_x, step_y):
    moved = packet
    if step_y != 0:
        moved = passed_along(moved.astype(jnp.bfloat16), "gy", -step_y).astype(moved.dtype)
    if step_x != 0:
        moved = passed_along(moved.astype(jnp.bfloat16), "gx", -step_x).astype(moved.dtype)
    return moved


def shards(
    features, weights, cotangent, send_lists, block_offset, block_input, block_output, block_count
):
    tiles = features[0, 0]
    tile_slots, voxels, channels = tiles.shape
    lists = send_lists[0, 0]
    halo_size = lists.shape[1]
    packets = tiles[lists]
    halo = jnp.stack(
        [travel(packets[which], pair[0], pair[1]) for which, pair in enumerate(DIRECTIONS)]
    )
    extended = jnp.concatenate([tiles, halo.reshape(8 * halo_size, voxels, channels)], axis=0)
    per_turn = 8
    block_slots = block_offset.shape[2]
    block_rows = block_input.shape[3]
    padded_slots = -(-block_slots // per_turn) * per_turn
    extra = padded_slots - block_slots
    used_blocks = block_count[0, 0]
    live = jnp.arange(padded_slots) < used_blocks
    offsets = jnp.pad(block_offset[0, 0], (0, extra))
    inputs = jnp.pad(block_input[0, 0], ((0, extra), (0, 0)))
    outputs = jnp.pad(block_output[0, 0], ((0, extra), (0, 0)), constant_values=tile_slots)
    outputs = jnp.where(live[:, None], outputs, tile_slots)
    turn_count = (used_blocks + per_turn - 1) // per_turn

    def slices(turn):
        start = turn * per_turn
        return (
            lax.dynamic_slice_in_dim(offsets, start, per_turn),
            lax.dynamic_slice_in_dim(inputs, start, per_turn),
            lax.dynamic_slice_in_dim(outputs, start, per_turn),
        )

    def forward_turn(turn, accum):
        turn_offsets, turn_inputs, turn_outputs = slices(turn)
        gathered = extended[turn_inputs.reshape(-1)].reshape(
            per_turn, block_rows * voxels, channels
        )
        product = jnp.einsum(
            "grc,gcd->grd", gathered, weights[turn_offsets], preferred_element_type=jnp.float32
        )
        return accum.at[turn_outputs.reshape(-1)].add(
            product.reshape(per_turn * block_rows, voxels, channels), mode="drop"
        )

    pre = lax.fori_loop(
        0, turn_count, forward_turn, jnp.zeros((tile_slots, voxels, channels), jnp.float32)
    )
    sigma = jax.nn.sigmoid(pre)
    out_features = (tiles.astype(jnp.float32) + pre * sigma).astype(jnp.bfloat16)
    incoming = cotangent[0, 0].astype(jnp.float32)
    pre_grad = (incoming * sigma * (1.0 + pre * (1.0 - sigma))).astype(jnp.bfloat16)
    padded_grad = jnp.concatenate(
        [pre_grad, jnp.zeros((1, voxels, channels), jnp.bfloat16)], axis=0
    )

    def backward_turn(turn, carry):
        ext_grad, weight_part = carry
        turn_offsets, turn_inputs, turn_outputs = slices(turn)
        gathered = extended[turn_inputs.reshape(-1)].reshape(
            per_turn, block_rows * voxels, channels
        )
        grads = padded_grad[turn_outputs.reshape(-1)].reshape(
            per_turn, block_rows * voxels, channels
        )
        mats = weights[turn_offsets]
        back = jnp.einsum("grd,gcd->grc", grads, mats, preferred_element_type=jnp.float32)
        ext_grad = ext_grad.at[turn_inputs.reshape(-1)].add(
            back.reshape(per_turn * block_rows, voxels, channels)
        )
        terms = jnp.einsum("grc,grd->gcd", gathered, grads, preferred_element_type=jnp.float32)
        weight_part = weight_part.at[turn_offsets].add(terms)
        return (ext_grad, weight_part)

    start = (
        jnp.zeros((tile_slots + 8 * halo_size, voxels, channels), jnp.float32),
        jnp.zeros(weights.shape, jnp.float32),
    )
    ext_grad, weight_part = lax.fori_loop(0, turn_count, backward_turn, start)
    adjoints = ext_grad[tile_slots:].reshape(8, halo_size, voxels, channels)
    returned = jnp.stack(
        [travel_back(adjoints[which], pair[0], pair[1]) for which, pair in enumerate(DIRECTIONS)]
    )
    feat_sum = incoming + ext_grad[:tile_slots]
    feat_sum = feat_sum.at[lists.reshape(-1)].add(returned.reshape(8 * halo_size, voxels, channels))
    feat_grad = feat_sum.astype(jnp.bfloat16)
    weight_total = lax.psum(weight_part, ("gx", "gy"))
    device_total = lax.axis_size("gx") * lax.axis_size("gy")
    weight_grad = weight_total / math.sqrt(voxels * tile_slots * device_total)
    return (out_features[None, None], feat_grad[None, None], weight_grad)


def solution(mesh):
    in_specs = (
        P("gx", "gy", None, None, None),
        P(),
        P("gx", "gy", None, None, None),
        P("gx", "gy", None, None),
        P("gx", "gy", None),
        P("gx", "gy", None, None),
        P("gx", "gy", None, None),
        P("gx", "gy"),
    )
    out_specs = (P("gx", "gy", None, None, None), P("gx", "gy", None, None, None), P())
    return jax.shard_map(shards, mesh=mesh, in_specs=in_specs, out_specs=out_specs, check_vma=False)
```

profile of v0, /device:TPU:1, one launch (start us, length us, event | category | flops | bytes accessed | tf_op | source)
XLA Modules:
  0.0 1024.6 jit_solution(5015731274001047856)
XLA Ops:
  19.4 5.1 collective-permute-start.7
  45.5 5.5 collective-permute-start.11
  54.7 5.9 collective-permute-done.9
  62.8 279.6 %while.22 = (s32[]{:T(128)}, f32[32,64,256]{2,1,0:T(8,128)S(1)}, s32[]{:T(128)}, s32[112,8]{1,0:T(8,128)S(1)}, s32[112,8]{1,0:T(8,128)S(1)}, /*index=5*/bf16[96,...) while((s32[]{:T(128)}, f32[32,64,256]{2,1,0:T(8,128)S(1)}, ...), condition=%wide.region_2.3_spmd, body=%wide.region_0.2_spmd.sunk | while | flops 537921920 | bytes 26226740 | solution.py:79
  74.0 8.8 scatter_fusion
  94.0 8.8 scatter_fusion
  113.9 8.8 scatter_fusion
  133.9 8.8 scatter_fusion
  153.9 8.8 scatter_fusion
  173.8 8.8 scatter_fusion
  193.8 8.8 scatter_fusion
  213.8 8.8 scatter_fusion
  233.7 8.8 scatter_fusion
  253.7 8.8 scatter_fusion
  273.7 8.8 scatter_fusion
  293.7 8.8 scatter_fusion
  313.6 8.8 scatter_fusion
  333.6 8.8 scatter_fusion
  353.4 480.4 %while.23 = (s32[]{:T(128)}, f32[96,64,256]{2,1,0:T(8,128)}, f32[27,256,256]{2,1,0:T(8,128)}, s32[]{:T(128)}, s32[112,8]{1,0:T(8,128)S(1)}, /*index=5*/s32[112,8...) while((s32[]{:T(128)}, f32[96,64,256]{2,1,0:T(8,128)}, ...), condition=%wide.region_6.7_spmd, body=%wide.region_3.6_spmd.sunk | while | flops 1075318144 | bytes 43008608 | solution.py:112
  361.9 13.5 %scatter_fusion.1 = f32[96,64,256]{2,1,0:T(8,128)} fusion(f32[96,64,256]{2,1,0:T(8,128)} %get-tuple-element.332, s32[64]{0:T(128)S(1)} %fusion.41, f32[64,64,256]{2,1,0:T(8,128)} %bitcast.112), kind=kCustom, calls=%fused_computation.7.clone.1 | custom fusion | flops 1048576 | bytes 12583168 | tf_op jit(solution)/shard_map/while/body/scatter-add | solution.py:101
  383.0 4.6 scatter_fusion.2
  396.0 13.5 %scatter_fusion.1 = f32[96,64,256]{2,1,0:T(8,128)} fusion(f32[96,64,256]{2,1,0:T(8,128)} %get-tuple-element.332, s32[64]{0:T(128)S(1)} %fusion.41, f32[64,64,256]{2,1,0:T(8,128)} %bitcast.112), kind=kCustom, calls=%fused_computation.7.clone.1 | custom fusion | flops 1048576 | bytes 12583168 | tf_op jit(solution)/shard_map/while/body/scatter-add | solution.py:101
  417.2 4.8 scatter_fusion.2
  430.4 13.5 %scatter_fusion.1 = f32[96,64,256]{2,1,0:T(8,128)} fusion(f32[96,64,256]{2,1,0:T(8,128)} %get-tuple-element.332, s32[64]{0:T(128)S(1)} %fusion.41, f32[64,64,256]{2,1,0:T(8,128)} %bitcast.112), kind=kCustom, calls=%fused_computation.7.clone.1 | custom fusion | flops 1048576 | bytes 12583168 | tf_op jit(solution)/shard_map/while/body/scatter-add | solution.py:101
  451.5 4.8 scatter_fusion.2
  464.7 13.5 %scatter_fusion.1 = f32[96,64,256]{2,1,0:T(8,128)} fusion(f32[96,64,256]{2,1,0:T(8,128)} %get-tuple-element.332, s32[64]{0:T(128)S(1)} %fusion.41, f32[64,64,256]{2,1,0:T(8,128)} %bitcast.112), kind=kCustom, calls=%fused_computation.7.clone.1 | custom fusion | flops 1048576 | bytes 12583168 | tf_op jit(solution)/shard_map/while/body/scatter-add | solution.py:101
  485.8 4.6 scatter_fusion.2
  498.9 13.4 %scatter_fusion.1 = f32[96,64,256]{2,1,0:T(8,128)} fusion(f32[96,64,256]{2,1,0:T(8,128)} %get-tuple-element.332, s32[64]{0:T(128)S(1)} %fusion.41, f32[64,64,256]{2,1,0:T(8,128)} %bitcast.112), kind=kCustom, calls=%fused_computation.7.clone.1 | custom fusion | flops 1048576 | bytes 12583168 | tf_op jit(solution)/shard_map/while/body/scatter-add | solution.py:101
  533.0 13.4 %scatter_fusion.1 = f32[96,64,256]{2,1,0:T(8,128)} fusion(f32[96,64,256]{2,1,0:T(8,128)} %get-tuple-element.332, s32[64]{0:T(128)S(1)} %fusion.41, f32[64,64,256]{2,1,0:T(8,128)} %bitcast.112), kind=kCustom, calls=%fused_computation.7.clone.1 | custom fusion | flops 1048576 | bytes 12583168 | tf_op jit(solution)/shard_map/while/body/scatter-add | solution.py:101
  554.0 4.7 scatter_fusion.2
  567.1 13.5 %scatter_fusion.1 = f32[96,64,256]{2,1,0:T(8,128)} fusion(f32[96,64,256]{2,1,0:T(8,128)} %get-tuple-element.332, s32[64]{0:T(128)S(1)} %fusion.41, f32[64,64,256]{2,1,0:T(8,128)} %bitcast.112), kind=kCustom, calls=%fused_computation.7.clone.1 | custom fusion | flops 1048576 | bytes 12583168 | tf_op jit(solution)/shard_map/while/body/scatter-add | solution.py:101
  601.3 13.6 %scatter_fusion.1 = f32[96,64,256]{2,1,0:T(8,128)} fusion(f32[96,64,256]{2,1,0:T(8,128)} %get-tuple-element.332, s32[64]{0:T(128)S(1)} %fusion.41, f32[64,64,256]{2,1,0:T(8,128)} %bitcast.112), kind=kCustom, calls=%fused_computation.7.clone.1 | custom fusion | flops 1048576 | bytes 12583168 | tf_op jit(solution)/shard_map/while/body/scatter-add | solution.py:101
  622.5 4.8 scatter_fusion.2
  635.7 13.6 %scatter_fusion.1 = f32[96,64,256]{2,1,0:T(8,128)} fusion(f32[96,64,256]{2,1,0:T(8,128)} %get-tuple-element.332, s32[64]{0:T(128)S(1)} %fusion.41, f32[64,64,256]{2,1,0:T(8,128)} %bitcast.112), kind=kCustom, calls=%fused_computation.7.clone.1 | custom fusion | flops 1048576 | bytes 12583168 | tf_op jit(solution)/shard_map/while/body/scatter-add | solution.py:101
  656.9 4.6 scatter_fusion.2
  670.0 13.6 %scatter_fusion.1 = f32[96,64,256]{2,1,0:T(8,128)} fusion(f32[96,64,256]{2,1,0:T(8,128)} %get-tuple-element.332, s32[64]{0:T(128)S(1)} %fusion.41, f32[64,64,256]{2,1,0:T(8,128)} %bitcast.112), kind=kCustom, calls=%fused_computation.7.clone.1 | custom fusion | flops 1048576 | bytes 12583168 | tf_op jit(solution)/shard_map/while/body/scatter-add | solution.py:101
  704.3 13.6 %scatter_fusion.1 = f32[96,64,256]{2,1,0:T(8,128)} fusion(f32[96,64,256]{2,1,0:T(8,128)} %get-tuple-element.332, s32[64]{0:T(128)S(1)} %fusion.41, f32[64,64,256]{2,1,0:T(8,128)} %bitcast.112), kind=kCustom, calls=%fused_computation.7.clone.1 | custom fusion | flops 1048576 | bytes 12583168 | tf_op jit(solution)/shard_map/while/body/scatter-add | solution.py:101
  725.5 4.7 scatter_fusion.2
  738.6 13.6 %scatter_fusion.1 = f32[96,64,256]{2,1,0:T(8,128)} fusion(f32[96,64,256]{2,1,0:T(8,128)} %get-tuple-element.332, s32[64]{0:T(128)S(1)} %fusion.41, f32[64,64,256]{2,1,0:T(8,128)} %bitcast.112), kind=kCustom, calls=%fused_computation.7.clone.1 | custom fusion | flops 1048576 | bytes 12583168 | tf_op jit(solution)/shard_map/while/body/scatter-add | solution.py:101
  759.8 4.8 scatter_fusion.2
  773.1 13.5 %scatter_fusion.1 = f32[96,64,256]{2,1,0:T(8,128)} fusion(f32[96,64,256]{2,1,0:T(8,128)} %get-tuple-element.332, s32[64]{0:T(128)S(1)} %fusion.41, f32[64,64,256]{2,1,0:T(8,128)} %bitcast.112), kind=kCustom, calls=%fused_computation.7.clone.1 | custom fusion | flops 1048576 | bytes 12583168 | tf_op jit(solution)/shard_map/while/body/scatter-add | solution.py:101
  794.2 4.7 scatter_fusion.2
  807.4 14.2 %scatter_fusion.1 = f32[96,64,256]{2,1,0:T(8,128)} fusion(f32[96,64,256]{2,1,0:T(8,128)} %get-tuple-element.332, s32[64]{0:T(128)S(1)} %fusion.41, f32[64,64,256]{2,1,0:T(8,128)} %bitcast.112), kind=kCustom, calls=%fused_computation.7.clone.1 | custom fusion | flops 1048576 | bytes 12583168 | tf_op jit(solution)/shard_map/while/body/scatter-add | solution.py:101
  862.0 6.8 collective-permute-done.19
  879.9 8.8 collective-permute-done.20
  894.3 8.8 scatter_fusion.3
  904.2 106.8 %all-reduce.6.cloned.1.call-done = f32[27,256,256]{2,1,0:T(8,128)} async-done(((f32[27,256,256]{2,1,0:T(8,128)}), f32[27,256,256]{2,1,0:T(8,128)}) %all-reduce.6.cloned.1.call-update) | async-done | bytes 7077904 | tf_op jit(solution)/shard_map/psum | solution.py:120
  1011.0 6.7 broadcast_multiply_fusion
  (459 shorter events, 493.7 us)
Async XLA Ops:
  7.2 1003.9 %all-reduce.6.cloned.1.call-start = ((), (), s32[]{:S(2)}) async-start(), calls=%async_computation | async-start | bytes 14155776 | tf_op jit(solution)/shard_map/psum | solution.py:120
  9.9 16.6 %copy-start.7 = (s32[1,1,108,8]{2,3,1,0:T(8,128)S(1)}, s32[1,1,108,8]{2,3,1,0:T(8,128)}, u32[]{:S(2)}) copy-start(s32[1,1,108,8]{2,3,1,0:T(8,128)} %param.18) | copy-start | bytes 10372
  9.9 16.8 %copy-start.8 = (s32[1,1,108,8]{2,3,1,0:T(8,128)S(1)}, s32[1,1,108,8]{2,3,1,0:T(8,128)}, u32[]{:S(2)}) copy-start(s32[1,1,108,8]{2,3,1,0:T(8,128)} %param.17) | copy-start | bytes 10372
  9.9 17.0 %copy-start.9 = (s32[1,1,108]{2,1,0:T(1,128)S(1)}, s32[1,1,108]{2,1,0:T(1,128)}, u32[]{:S(2)}) copy-start(s32[1,1,108]{2,1,0:T(1,128)} %param.16) | copy-start | bytes 1300
  11.0 14.2 %collective-permute-start = (bf16[8,64,256]{2,1,0:T(8,128)(2,1)S(1)}, bf16[8,64,256]{2,1,0:T(8,128)(2,1)S(1)}, u32[]{:S(2)}, u32[]{:S(2)}) collective-permute-start(bf16[8,64,256]{2,1,0:T(8,128)(2,1)S(1)} %get-tuple-element.160), channel_id=1, source_target_pairs={{8,0},{16,8},{24,16},{32,24},{40,32},{48,40},{56,48},{64,56},{72,6... | collective-permute-start | bytes 786440 | tf_op jit(solution)/shard_map/ppermute | solution.py:13
  14.2 22.7 %collective-permute-start.2 = (bf16[8,64,256]{2,1,0:T(8,128)(2,1)}, bf16[8,64,256]{2,1,0:T(8,128)(2,1)S(1)}, u32[]{:S(2)}, u32[]{:S(2)}) collective-permute-start(bf16[8,64,256]{2,1,0:T(8,128)(2,1)} %get-tuple-element.159), channel_id=1, source_target_pairs={{8,0},{16,8},{24,16},{32,24},{40,32},{48,40},{56,48},{64,56},{72,6... | collective-permute-start | bytes 786440 | tf_op jit(solution)/shard_map/ppermute | solution.py:13
  16.2 10.7 %collective-permute-start.3 = (bf16[8,64,256]{2,1,0:T(8,128)(2,1)}, bf16[8,64,256]{2,1,0:T(8,128)(2,1)S(1)}, u32[]{:S(2)}, u32[]{:S(2)}) collective-permute-start(bf16[8,64,256]{2,1,0:T(8,128)(2,1)} %get-tuple-element.158), channel_id=1, source_target_pairs={{8,0},{16,8},{24,16},{32,24},{40,32},{48,40},{56,48},{64,56},{72,6... | collective-permute-start | bytes 786440 | tf_op jit(solution)/shard_map/ppermute | solution.py:13
  18.1 32.9 %collective-permute-start.5 = (bf16[8,64,256]{2,1,0:T(8,128)(2,1)S(1)}, bf16[8,64,256]{2,1,0:T(8,128)(2,1)S(1)}, u32[]{:S(2)}, u32[]{:S(2)}) collective-permute-start(bf16[8,64,256]{2,1,0:T(8,128)(2,1)S(1)} %get-tuple-element.157), channel_id=1, source_target_pairs={{1,0},{2,1},{3,2},{4,3},{5,4},{6,5},{7,6},{9,8},{10,9},{11,10},{12... | collective-permute-start | bytes 786440 | tf_op jit(solution)/shard_map/ppermute | solution.py:13
  19.4 20.8 %collective-permute-start.7 = (bf16[8,64,256]{2,1,0:T(8,128)(2,1)S(1)}, bf16[8,64,256]{2,1,0:T(8,128)(2,1)S(1)}, u32[]{:S(2)}, u32[]{:S(2)}) collective-permute-start(bf16[8,64,256]{2,1,0:T(8,128)(2,1)S(1)} %get-tuple-element.155), channel_id=1, source_target_pairs={{0,8},{8,16},{16,24},{24,32},{32,40},{40,48},{48,56},{56,64},{64,7... | collective-permute-start | bytes 786440 | tf_op jit(solution)/shard_map/ppermute | solution.py:13
  25.2 8.0 collective-permute-start.1
  26.9 33.8 %copy-start = (bf16[1,1,32,64,256]{4,3,2,1,0:T(8,128)(2,1)S(1)}, bf16[1,1,32,64,256]{4,3,2,1,0:T(8,128)(2,1)}, u32[]{:S(2)}) copy-start(bf16[1,1,32,64,256]{4,3,2,1,0:T(8,128)(2,1)} %param.12) | copy-start | bytes 3145732
  26.9 17.2 %collective-permute-start.10 = (bf16[8,64,256]{2,1,0:T(8,128)(2,1)S(1)}, bf16[8,64,256]{2,1,0:T(8,128)(2,1)S(1)}, u32[]{:S(2)}, u32[]{:S(2)}) collective-permute-start(bf16[8,64,256]{2,1,0:T(8,128)(2,1)S(1)} %get-tuple-element.153), channel_id=1, source_target_pairs={{0,8},{8,16},{16,24},{24,32},{32,40},{40,48},{48,56},{56,64},{64,7... | collective-permute-start | bytes 786440 | tf_op jit(solution)/shard_map/ppermute | solution.py:13
  33.2 12.2 %collective-permute-start.4 = (bf16[8,64,256]{2,1,0:T(8,128)(2,1)S(1)}, bf16[8,64,256]{2,1,0:T(8,128)(2,1)S(1)}, u32[]{:S(2)}, u32[]{:S(2)}) collective-permute-start(bf16[8,64,256]{2,1,0:T(8,128)(2,1)S(1)} %collective-permute-done.3), channel_id=1, source_target_pairs={{0,1},{1,2},{2,3},{3,4},{4,5},{5,6},{6,7},{8,9},{9,10},{10,11},{11... | collective-permute-start | bytes 786440 | tf_op jit(solution)/shard_map/ppermute | solution.py:13
  36.9 14.1 %collective-permute-start.6 = (bf16[8,64,256]{2,1,0:T(8,128)(2,1)S(1)}, bf16[8,64,256]{2,1,0:T(8,128)(2,1)S(1)}, u32[]{:S(2)}, u32[]{:S(2)}) collective-permute-start(bf16[8,64,256]{2,1,0:T(8,128)(2,1)S(1)} %get-tuple-element.156), channel_id=1, source_target_pairs={{0,1},{1,2},{2,3},{3,4},{4,5},{5,6},{6,7},{8,9},{9,10},{10,11},{11... | collective-permute-start | bytes 786440 | tf_op jit(solution)/shard_map/ppermute | solution.py:13
  40.2 20.5 %collective-permute-start.9 = (bf16[8,64,256]{2,1,0:T(8,128)(2,1)S(1)}, bf16[8,64,256]{2,1,0:T(8,128)(2,1)S(1)}, u32[]{:S(2)}, u32[]{:S(2)}) collective-permute-start(bf16[8,64,256]{2,1,0:T(8,128)(2,1)S(1)} %get-tuple-element.154), channel_id=1, source_target_pairs={{0,8},{8,16},{16,24},{24,32},{32,40},{40,48},{48,56},{56,64},{64,7... | collective-permute-start | bytes 786440 | tf_op jit(solution)/shard_map/ppermute | solution.py:13
  44.2 10.5 %collective-permute-start.8 = (bf16[8,64,256]{2,1,0:T(8,128)(2,1)S(1)}, bf16[8,64,256]{2,1,0:T(8,128)(2,1)S(1)}, u32[]{:S(2)}, u32[]{:S(2)}) collective-permute-start(bf16[8,64,256]{2,1,0:T(8,128)(2,1)S(1)} %collective-permute-done.7), channel_id=1, source_target_pairs={{1,0},{2,1},{3,2},{4,3},{5,4},{6,5},{7,6},{9,8},{10,9},{11,10},{12... | collective-permute-start | bytes 786440 | tf_op jit(solution)/shard_map/ppermute | solution.py:13
  45.5 15.2 %collective-permute-start.11 = (bf16[8,64,256]{2,1,0:T(8,128)(2,1)S(1)}, bf16[8,64,256]{2,1,0:T(8,128)(2,1)S(1)}, u32[]{:S(2)}, u32[]{:S(2)}) collective-permute-start(bf16[8,64,256]{2,1,0:T(8,128)(2,1)S(1)} %collective-permute-done.10), channel_id=1, source_target_pairs={{0,1},{1,2},{2,3},{3,4},{4,5},{5,6},{6,7},{8,9},{9,10},{10,11},{11... | collective-permute-start | bytes 786440 | tf_op jit(solution)/shard_map/ppermute | solution.py:13
  837.1 3.2 copy-start.6
  837.1 9.8 copy-start.1
  838.2 6.7 collective-permute-start.12
  840.3 20.3 %collective-permute-start.14 = (bf16[8,64,256]{2,1,0:T(8,128)(2,1)}, bf16[8,64,256]{2,1,0:T(8,128)(2,1)S(1)}, u32[]{:S(2)}, u32[]{:S(2)}) collective-permute-start(bf16[8,64,256]{2,1,0:T(8,128)(2,1)} %get-tuple-element.149), channel_id=1, source_target_pairs={{0,8},{8,16},{16,24},{24,32},{32,40},{40,48},{48,56},{56,64},{64,7... | collective-permute-start | bytes 786440 | tf_op jit(solution)/shard_map/ppermute | solution.py:13
  842.2 6.5 copy-start.3
  842.3 10.5 %copy-start.5 = (bf16[8,64,256]{2,1,0:T(8,128)(2,1)S(1)}, bf16[8,64,256]{2,1,0:T(8,128)(2,1)}, u32[]{:S(2)}) copy-start(bf16[8,64,256]{2,1,0:T(8,128)(2,1)} %get-tuple-element.145) | copy-start | bytes 786436
  842.3 12.7 %copy-start.4 = (bf16[8,64,256]{2,1,0:T(8,128)(2,1)S(1)}, bf16[8,64,256]{2,1,0:T(8,128)(2,1)}, u32[]{:S(2)}) copy-start(bf16[8,64,256]{2,1,0:T(8,128)(2,1)} %get-tuple-element.143) | copy-start | bytes 786436
  842.3 18.4 %copy-start.2 = (bf16[8,64,256]{2,1,0:T(8,128)(2,1)S(1)}, bf16[8,64,256]{2,1,0:T(8,128)(2,1)}, u32[]{:S(2)}) copy-start(bf16[8,64,256]{2,1,0:T(8,128)(2,1)} %get-tuple-element.146) | copy-start | bytes 786436
  842.3 12.6 %collective-permute-start.15 = (bf16[8,64,256]{2,1,0:T(8,128)(2,1)}, bf16[8,64,256]{2,1,0:T(8,128)(2,1)S(1)}, u32[]{:S(2)}, u32[]{:S(2)}) collective-permute-start(bf16[8,64,256]{2,1,0:T(8,128)(2,1)} %get-tuple-element.148), channel_id=1, source_target_pairs={{1,0},{2,1},{3,2},{4,3},{5,4},{6,5},{7,6},{9,8},{10,9},{11,10},{12... | collective-permute-start | bytes 786440 | tf_op jit(solution)/shard_map/ppermute | solution.py:13
  844.9 11.3 %collective-permute-start.13 = (bf16[8,64,256]{2,1,0:T(8,128)(2,1)}, bf16[8,64,256]{2,1,0:T(8,128)(2,1)S(1)}, u32[]{:S(2)}, u32[]{:S(2)}) collective-permute-start(bf16[8,64,256]{2,1,0:T(8,128)(2,1)} %collective-permute-done.12), channel_id=1, source_target_pairs={{0,8},{8,16},{16,24},{24,32},{32,40},{40,48},{48,56},{56,64},{64,7... | collective-permute-start | bytes 786440 | tf_op jit(solution)/shard_map/ppermute | solution.py:13
  848.8 28.7 %collective-permute-start.17 = (bf16[8,64,256]{2,1,0:T(8,128)(2,1)S(1)}, bf16[8,64,256]{2,1,0:T(8,128)(2,1)S(1)}, u32[]{:S(2)}, u32[]{:S(2)}) collective-permute-start(bf16[8,64,256]{2,1,0:T(8,128)(2,1)S(1)} %copy-done.3), channel_id=1, source_target_pairs={{0,1},{1,2},{2,3},{3,4},{4,5},{5,6},{6,7},{8,9},{9,10},{10,11},{11... | collective-permute-start | bytes 786440 | tf_op jit(solution)/shard_map/ppermute | solution.py:13
  852.7 16.1 %collective-permute-start.19 = (bf16[8,64,256]{2,1,0:T(8,128)(2,1)S(1)}, bf16[8,64,256]{2,1,0:T(8,128)(2,1)S(1)}, u32[]{:S(2)}, u32[]{:S(2)}) collective-permute-start(bf16[8,64,256]{2,1,0:T(8,128)(2,1)S(1)} %copy-done.5), channel_id=1, source_target_pairs={{0,1},{1,2},{2,3},{3,4},{4,5},{5,6},{6,7},{8,9},{9,10},{10,11},{11... | collective-permute-start | bytes 786440 | tf_op jit(solution)/shard_map/ppermute | solution.py:13
  854.9 17.3 %collective-permute-start.22 = (bf16[8,64,256]{2,1,0:T(8,128)(2,1)S(1)}, bf16[8,64,256]{2,1,0:T(8,128)(2,1)S(1)}, u32[]{:S(2)}, u32[]{:S(2)}) collective-permute-start(bf16[8,64,256]{2,1,0:T(8,128)(2,1)S(1)} %copy-done.4), channel_id=1, source_target_pairs={{1,0},{2,1},{3,2},{4,3},{5,4},{6,5},{7,6},{9,8},{10,9},{11,10},{12... | collective-permute-start | bytes 786440 | tf_op jit(solution)/shard_map/ppermute | solution.py:13
  856.2 19.3 %collective-permute-start.16 = (bf16[8,64,256]{2,1,0:T(8,128)(2,1)S(1)}, bf16[8,64,256]{2,1,0:T(8,128)(2,1)S(1)}, u32[]{:S(2)}, u32[]{:S(2)}) collective-permute-start(bf16[8,64,256]{2,1,0:T(8,128)(2,1)S(1)} %collective-permute-done.15), channel_id=1, source_target_pairs={{0,8},{8,16},{16,24},{24,32},{32,40},{40,48},{48,56},{56,64},{64,7... | collective-permute-start | bytes 786440 | tf_op jit(solution)/shard_map/ppermute | solution.py:13
  860.6 19.3 %collective-permute-start.18 = (bf16[8,64,256]{2,1,0:T(8,128)(2,1)S(1)}, bf16[8,64,256]{2,1,0:T(8,128)(2,1)S(1)}, u32[]{:S(2)}, u32[]{:S(2)}) collective-permute-start(bf16[8,64,256]{2,1,0:T(8,128)(2,1)S(1)} %copy-done.2), channel_id=1, source_target_pairs={{1,0},{2,1},{3,2},{4,3},{5,4},{6,5},{7,6},{9,8},{10,9},{11,10},{12... | collective-permute-start | bytes 786440 | tf_op jit(solution)/shard_map/ppermute | solution.py:13
  868.8 19.9 %collective-permute-start.21 = (bf16[8,64,256]{2,1,0:T(8,128)(2,1)S(1)}, bf16[8,64,256]{2,1,0:T(8,128)(2,1)S(1)}, u32[]{:S(2)}, u32[]{:S(2)}) collective-permute-start(bf16[8,64,256]{2,1,0:T(8,128)(2,1)S(1)} %get-tuple-element.144), channel_id=1, source_target_pairs={{8,0},{16,8},{24,16},{32,24},{40,32},{48,40},{56,48},{64,56},{72,6... | collective-permute-start | bytes 786440 | tf_op jit(solution)/shard_map/ppermute | solution.py:13
  872.3 16.4 %collective-permute-start.20 = (bf16[8,64,256]{2,1,0:T(8,128)(2,1)S(1)}, bf16[8,64,256]{2,1,0:T(8,128)(2,1)S(1)}, u32[]{:S(2)}, u32[]{:S(2)}) collective-permute-start(bf16[8,64,256]{2,1,0:T(8,128)(2,1)S(1)} %collective-permute-done.19), channel_id=1, source_target_pairs={{8,0},{16,8},{24,16},{32,24},{40,32},{48,40},{56,48},{64,56},{72,6... | collective-permute-start | bytes 786440 | tf_op jit(solution)/shard_map/ppermute | solution.py:13
  875.5 16.0 %collective-permute-start.23 = (bf16[8,64,256]{2,1,0:T(8,128)(2,1)S(1)}, bf16[8,64,256]{2,1,0:T(8,128)(2,1)S(1)}, u32[]{:S(2)}, u32[]{:S(2)}) collective-permute-start(bf16[8,64,256]{2,1,0:T(8,128)(2,1)S(1)} %collective-permute-done.22), channel_id=1, source_target_pairs={{8,0},{16,8},{24,16},{32,24},{40,32},{48,40},{56,48},{64,56},{72,6... | collective-permute-start | bytes 786440 | tf_op jit(solution)/shard_map/ppermute | solution.py:13
Sparse Core Ops, SparseCore 0:
  833.9 177.0 all-reduce.5
where the time goes:
time: 1030 us; the launch traced here: 1020 us
  other arithmetic  412 us (40%)
  local copies, waits for them, and re-layouts  223 us (22%)
  matrix products  167 us (16%)
  waiting for transfers between devices  142 us (14%)
  starting transfers between devices  63.9 us (6%)
  between operations  15.4 us (1%)
    scatter-add x14, other arithmetic, backward_turn(): ext_grad.at[turn_inputs.reshape(-1)]  190 us
    scatter-add x14, other arithmetic, forward_turn(): accum.at[turn_outputs.reshape(-1)]  123 us
    psum x1, waiting for transfers between devices, shards(): weight_total = lax.psum(weight_part, ('gx', 'gy'))  107 us
    scatter-add x14, other arithmetic, backward_turn(): weight_part = weight_part.at[turn_offsets].add(terms)  65.3 us
    ppermute x24, starting transfers between devices, passed_along(): return lax.ppermute(x, axis, pairs)  63.8 us
    dot_general x14, matrix products, forward_turn(): jnp.einsum('grc,gcd->grd', gathered, weights[turn_offsets], preferred_ele...  60.4 us
    dot_general x14, matrix products, backward_turn(): jnp.einsum('grd,gcd->grc', grads, mats, preferred_element_type=jnp.float32)  55 us
    gather x14, local copies, waits for them, and re-layouts, forward_turn(): extended[turn_inputs.reshape(-1)]  54.7 us
  transfers between devices with their start and end apart: 25, of which 9 were waited for; matrix products, arithmetic and copies ran while one was open for 2% of the time, Pallas kernels for 0%

commit v1 on v0

--- a/solution.py
+++ b/solution.py
@@ -5,6 +5,10 @@
 from jax.sharding import PartitionSpec as P
 
 DIRECTIONS = ((-1, -1), (-1, 0), (-1, 1), (0, -1), (0, 1), (1, -1), (1, 0), (1, 1))
+
+
+def _use_levels_all(z, lane_axis, dev_axis="gx"):
+    return lax.psum(lax.psum(z, lane_axis), dev_axis)
 
 
 def passed_along(x, axis, by):
@@ -117,7 +121,7 @@
     feat_sum = incoming + ext_grad[:tile_slots]
     feat_sum = feat_sum.at[lists.reshape(-1)].add(returned.reshape(8 * halo_size, voxels, channels))
     feat_grad = feat_sum.astype(jnp.bfloat16)
-    weight_total = lax.psum(weight_part, ("gx", "gy"))
+    weight_total = _use_levels_all(weight_part, "gy")
     device_total = lax.axis_size("gx") * lax.axis_size("gy")
     weight_grad = weight_total / math.sqrt(voxels * tile_slots * device_total)
     return (out_features[None, None], feat_grad[None, None], weight_grad)

time: 1030 us -> 1220 us (1.18)
  waiting for transfers between devices: 142 us -> 325 us
    psum x1 -> x2, waiting for transfers between devices: 107 us -> 268 us  [_use_levels_all(): return lax.psum(lax.psum(z, lane_axis), dev_axis)]
    ppermute x24, waiting for transfers between devices: 35.3 us -> 57.2 us  [passed_along(): return lax.ppermute(x, axis, pairs)]
  transfers between devices with their start and end apart: 25 -> 26, of which waited for: 9 -> 9; matrix products, arithmetic and copies ran while one was open for 2% -> 2% of each run, Pallas kernels for 0% -> 0%
where the time goes in v1:
time: 1220 us; the launch traced here: 1210 us
  other arithmetic  412 us (34%)
  waiting for transfers between devices  325 us (27%)
  local copies, waits for them, and re-layouts  223 us (18%)
  matrix products  167 us (14%)
  starting transfers between devices  68.3 us (6%)
  between operations  15.4 us (1%)
    psum x2, waiting for transfers between devices, _use_levels_all(): return lax.psum(lax.psum(z, lane_axis), dev_axis)  268 us
    scatter-add x14, other arithmetic, backward_turn(): ext_grad.at[turn_inputs.reshape(-1)]  190 us
    scatter-add x14, other arithmetic, forward_turn(): accum.at[turn_outputs.reshape(-1)]  123 us
    ppermute x24, starting transfers between devices, passed_along(): return lax.ppermute(x, axis, pairs)  68.2 us
    scatter-add x14, other arithmetic, backward_turn(): weight_part = weight_part.at[turn_offsets].add(terms)  65.2 us
    dot_general x14, matrix products, forward_turn(): jnp.einsum('grc,gcd->grd', gathered, weights[turn_offsets], preferred_ele...  60.4 us
    ppermute x24, waiting for transfers between devices, passed_along(): return lax.ppermute(x, axis, pairs)  57.2 us
    dot_general x14, matrix products, backward_turn(): jnp.einsum('grd,gcd->grc', grads, mats, preferred_element_type=jnp.float32)  55 us
  transfers between devices with their start and end apart: 26, of which 9 were waited for; matrix products, arithmetic and copies ran while one was open for 2% of the time, Pallas kernels for 0%

profile of v1, /device:TPU:1, one launch (start us, length us, event | category | flops | bytes accessed | tf_op | source)
XLA Modules:
  0.0 1211.7 jit_solution(3663239895401281881)
XLA Ops:
  19.4 5.1 collective-permute-start.7
  45.5 5.5 collective-permute-start.11
  54.7 5.9 collective-permute-done.9
  62.9 279.6 %while.22 = (s32[]{:T(128)}, f32[32,64,256]{2,1,0:T(8,128)S(1)}, s32[]{:T(128)}, s32[112,8]{1,0:T(8,128)S(1)}, s32[112,8]{1,0:T(8,128)S(1)}, /*index=5*/bf16[96,...) while((s32[]{:T(128)}, f32[32,64,256]{2,1,0:T(8,128)S(1)}, ...), condition=%wide.region_2.3_spmd, body=%wide.region_0.2_spmd.sunk | while | flops 537921920 | bytes 26226740 | solution.py:83
  74.1 8.8 scatter_fusion
  94.0 8.8 scatter_fusion
  114.0 8.8 scatter_fusion
  134.0 8.8 scatter_fusion
  153.9 8.8 scatter_fusion
  173.9 8.8 scatter_fusion
  193.9 8.8 scatter_fusion
  213.9 8.8 scatter_fusion
  233.8 8.8 scatter_fusion
  253.8 8.8 scatter_fusion
  273.8 8.8 scatter_fusion
  293.7 8.8 scatter_fusion
  313.7 8.8 scatter_fusion
  333.7 8.8 scatter_fusion
  353.4 480.0 %while.23 = (s32[]{:T(128)}, f32[96,64,256]{2,1,0:T(8,128)}, f32[27,256,256]{2,1,0:T(8,128)}, s32[]{:T(128)}, s32[112,8]{1,0:T(8,128)S(1)}, /*index=5*/s32[112,8...) while((s32[]{:T(128)}, f32[96,64,256]{2,1,0:T(8,128)}, ...), condition=%wide.region_6.7_spmd, body=%wide.region_3.6_spmd.sunk | while | flops 1075318144 | bytes 43008608 | solution.py:116
  361.8 13.5 %scatter_fusion.1 = f32[96,64,256]{2,1,0:T(8,128)} fusion(f32[96,64,256]{2,1,0:T(8,128)} %get-tuple-element.332, s32[64]{0:T(128)S(1)} %fusion.41, f32[64,64,256]{2,1,0:T(8,128)} %bitcast.112), kind=kCustom, calls=%fused_computation.7.clone.1 | custom fusion | flops 1048576 | bytes 12583168 | tf_op jit(solution)/shard_map/while/body/scatter-add | solution.py:105
  382.9 4.7 scatter_fusion.2
  396.1 13.5 %scatter_fusion.1 = f32[96,64,256]{2,1,0:T(8,128)} fusion(f32[96,64,256]{2,1,0:T(8,128)} %get-tuple-element.332, s32[64]{0:T(128)S(1)} %fusion.41, f32[64,64,256]{2,1,0:T(8,128)} %bitcast.112), kind=kCustom, calls=%fused_computation.7.clone.1 | custom fusion | flops 1048576 | bytes 12583168 | tf_op jit(solution)/shard_map/while/body/scatter-add | solution.py:105
  417.2 4.8 scatter_fusion.2
  430.5 13.5 %scatter_fusion.1 = f32[96,64,256]{2,1,0:T(8,128)} fusion(f32[96,64,256]{2,1,0:T(8,128)} %get-tuple-element.332, s32[64]{0:T(128)S(1)} %fusion.41, f32[64,64,256]{2,1,0:T(8,128)} %bitcast.112), kind=kCustom, calls=%fused_computation.7.clone.1 | custom fusion | flops 1048576 | bytes 12583168 | tf_op jit(solution)/shard_map/while/body/scatter-add | solution.py:105
  464.6 13.5 %scatter_fusion.1 = f32[96,64,256]{2,1,0:T(8,128)} fusion(f32[96,64,256]{2,1,0:T(8,128)} %get-tuple-element.332, s32[64]{0:T(128)S(1)} %fusion.41, f32[64,64,256]{2,1,0:T(8,128)} %bitcast.112), kind=kCustom, calls=%fused_computation.7.clone.1 | custom fusion | flops 1048576 | bytes 12583168 | tf_op jit(solution)/shard_map/while/body/scatter-add | solution.py:105
  498.8 13.4 %scatter_fusion.1 = f32[96,64,256]{2,1,0:T(8,128)} fusion(f32[96,64,256]{2,1,0:T(8,128)} %get-tuple-element.332, s32[64]{0:T(128)S(1)} %fusion.41, f32[64,64,256]{2,1,0:T(8,128)} %bitcast.112), kind=kCustom, calls=%fused_computation.7.clone.1 | custom fusion | flops 1048576 | bytes 12583168 | tf_op jit(solution)/shard_map/while/body/scatter-add | solution.py:105
  533.0 13.4 %scatter_fusion.1 = f32[96,64,256]{2,1,0:T(8,128)} fusion(f32[96,64,256]{2,1,0:T(8,128)} %get-tuple-element.332, s32[64]{0:T(128)S(1)} %fusion.41, f32[64,64,256]{2,1,0:T(8,128)} %bitcast.112), kind=kCustom, calls=%fused_computation.7.clone.1 | custom fusion | flops 1048576 | bytes 12583168 | tf_op jit(solution)/shard_map/while/body/scatter-add | solution.py:105
  554.0 4.7 scatter_fusion.2
  567.2 13.4 %scatter_fusion.1 = f32[96,64,256]{2,1,0:T(8,128)} fusion(f32[96,64,256]{2,1,0:T(8,128)} %get-tuple-element.332, s32[64]{0:T(128)S(1)} %fusion.41, f32[64,64,256]{2,1,0:T(8,128)} %bitcast.112), kind=kCustom, calls=%fused_computation.7.clone.1 | custom fusion | flops 1048576 | bytes 12583168 | tf_op jit(solution)/shard_map/while/body/scatter-add | solution.py:105
  601.3 13.6 %scatter_fusion.1 = f32[96,64,256]{2,1,0:T(8,128)} fusion(f32[96,64,256]{2,1,0:T(8,128)} %get-tuple-element.332, s32[64]{0:T(128)S(1)} %fusion.41, f32[64,64,256]{2,1,0:T(8,128)} %bitcast.112), kind=kCustom, calls=%fused_computation.7.clone.1 | custom fusion | flops 1048576 | bytes 12583168 | tf_op jit(solution)/shard_map/while/body/scatter-add | solution.py:105
  635.6 13.5 %scatter_fusion.1 = f32[96,64,256]{2,1,0:T(8,128)} fusion(f32[96,64,256]{2,1,0:T(8,128)} %get-tuple-element.332, s32[64]{0:T(128)S(1)} %fusion.41, f32[64,64,256]{2,1,0:T(8,128)} %bitcast.112), kind=kCustom, calls=%fused_computation.7.clone.1 | custom fusion | flops 1048576 | bytes 12583168 | tf_op jit(solution)/shard_map/while/body/scatter-add | solution.py:105
  656.7 4.7 scatter_fusion.2
  669.9 13.6 %scatter_fusion.1 = f32[96,64,256]{2,1,0:T(8,128)} fusion(f32[96,64,256]{2,1,0:T(8,128)} %get-tuple-element.332, s32[64]{0:T(128)S(1)} %fusion.41, f32[64,64,256]{2,1,0:T(8,128)} %bitcast.112), kind=kCustom, calls=%fused_computation.7.clone.1 | custom fusion | flops 1048576 | bytes 12583168 | tf_op jit(solution)/shard_map/while/body/scatter-add | solution.py:105
  691.1 4.7 scatter_fusion.2
  704.2 13.6 %scatter_fusion.1 = f32[96,64,256]{2,1,0:T(8,128)} fusion(f32[96,64,256]{2,1,0:T(8,128)} %get-tuple-element.332, s32[64]{0:T(128)S(1)} %fusion.41, f32[64,64,256]{2,1,0:T(8,128)} %bitcast.112), kind=kCustom, calls=%fused_computation.7.clone.1 | custom fusion | flops 1048576 | bytes 12583168 | tf_op jit(solution)/shard_map/while/body/scatter-add | solution.py:105
  738.5 13.6 %scatter_fusion.1 = f32[96,64,256]{2,1,0:T(8,128)} fusion(f32[96,64,256]{2,1,0:T(8,128)} %get-tuple-element.332, s32[64]{0:T(128)S(1)} %fusion.41, f32[64,64,256]{2,1,0:T(8,128)} %bitcast.112), kind=kCustom, calls=%fused_computation.7.clone.1 | custom fusion | flops 1048576 | bytes 12583168 | tf_op jit(solution)/shard_map/while/body/scatter-add | solution.py:105
  772.7 13.6 %scatter_fusion.1 = f32[96,64,256]{2,1,0:T(8,128)} fusion(f32[96,64,256]{2,1,0:T(8,128)} %get-tuple-element.332, s32[64]{0:T(128)S(1)} %fusion.41, f32[64,64,256]{2,1,0:T(8,128)} %bitcast.112), kind=kCustom, calls=%fused_computation.7.clone.1 | custom fusion | flops 1048576 | bytes 12583168 | tf_op jit(solution)/shard_map/while/body/scatter-add | solution.py:105
  807.0 14.0 %scatter_fusion.1 = f32[96,64,256]{2,1,0:T(8,128)} fusion(f32[96,64,256]{2,1,0:T(8,128)} %get-tuple-element.332, s32[64]{0:T(128)S(1)} %fusion.41, f32[64,64,256]{2,1,0:T(8,128)} %bitcast.112), kind=kCustom, calls=%fused_computation.7.clone.1 | custom fusion | flops 1048576 | bytes 12583168 | tf_op jit(solution)/shard_map/while/body/scatter-add | solution.py:105
  828.6 4.8 scatter_fusion.2
  833.5 162.7 %all-reduce.7.cloned.1.call-done = f32[27,256,256]{2,1,0:T(8,128)} async-done(((f32[27,256,256]{2,1,0:T(8,128)}), f32[27,256,256]{2,1,0:T(8,128)}) %all-reduce.7.cloned.1.call-update) | async-done | bytes 7077904 | tf_op jit(solution)/shard_map/psum | solution.py:11
  1002.7 5.4 collective-permute-start.14
  1023.0 15.7 %collective-permute-done.13 = bf16[8,64,256]{2,1,0:T(8,128)(2,1)S(1)} collective-permute-done((bf16[8,64,256]{2,1,0:T(8,128)(2,1)}, bf16[8,64,256]{2,1,0:T(8,128)(2,1)S(1)}, u32[]{:S(2)}, u32[]{:S(2)}) %collective-permute-start.13) | collective-permute-done | bytes 262176 | tf_op jit(solution)/shard_map/ppermute | solution.py:17
  1038.7 6.0 collective-permute-start.16
  1055.1 16.5 %collective-permute-done.20 = bf16[8,64,256]{2,1,0:T(8,128)(2,1)S(1)} collective-permute-done((bf16[8,64,256]{2,1,0:T(8,128)(2,1)S(1)}, bf16[8,64,256]{2,1,0:T(8,128)(2,1)S(1)}, u32[]{:S(2)}, u32[]{:S(2)}) %collective-permute-start.20) | collective-permute-done | bytes 262176 | tf_op jit(solution)/shard_map/ppermute | solution.py:17
  1071.7 8.4 collective-permute-done.23
  1082.8 8.9 scatter_fusion.3
  1092.8 105.4 %all-reduce.9.cloned.1.call-done = f32[27,256,256]{2,1,0:T(8,128)} async-done(((f32[27,256,256]{2,1,0:T(8,128)}), f32[27,256,256]{2,1,0:T(8,128)}) %all-reduce.9.cloned.1.call-update) | async-done | bytes 7077904 | tf_op jit(solution)/shard_map/psum | solution.py:11
  1198.2 6.7 broadcast_multiply_fusion
  (462 shorter events, 501.9 us)
Async XLA Ops:
  7.2 989.0 %all-reduce.7.cloned.1.call-start = ((), (), s32[]{:S(2)}) async-start(), calls=%async_computation | async-start | bytes 14155776 | tf_op jit(solution)/shard_map/psum | solution.py:11
  9.9 16.6 %copy-start.7 = (s32[1,1,108,8]{2,3,1,0:T(8,128)S(1)}, s32[1,1,108,8]{2,3,1,0:T(8,128)}, u32[]{:S(2)}) copy-start(s32[1,1,108,8]{2,3,1,0:T(8,128)} %param.18) | copy-start | bytes 10372
  9.9 16.8 %copy-start.8 = (s32[1,1,108,8]{2,3,1,0:T(8,128)S(1)}, s32[1,1,108,8]{2,3,1,0:T(8,128)}, u32[]{:S(2)}) copy-start(s32[1,1,108,8]{2,3,1,0:T(8,128)} %param.17) | copy-start | bytes 10372
  9.9 17.0 %copy-start.9 = (s32[1,1,108]{2,1,0:T(1,128)S(1)}, s32[1,1,108]{2,1,0:T(1,128)}, u32[]{:S(2)}) copy-start(s32[1,1,108]{2,1,0:T(1,128)} %param.16) | copy-start | bytes 1300
  11.0 14.2 %collective-permute-start = (bf16[8,64,256]{2,1,0:T(8,128)(2,1)S(1)}, bf16[8,64,256]{2,1,0:T(8,128)(2,1)S(1)}, u32[]{:S(2)}, u32[]{:S(2)}) collective-permute-start(bf16[8,64,256]{2,1,0:T(8,128)(2,1)S(1)} %get-tuple-element.160), channel_id=1, source_target_pairs={{8,0},{16,8},{24,16},{32,24},{40,32},{48,40},{56,48},{64,56},{72,6... | collective-permute-start | bytes 786440 | tf_op jit(solution)/shard_map/ppermute | solution.py:17
  14.2 22.7 %collective-permute-start.2 = (bf16[8,64,256]{2,1,0:T(8,128)(2,1)}, bf16[8,64,256]{2,1,0:T(8,128)(2,1)S(1)}, u32[]{:S(2)}, u32[]{:S(2)}) collective-permute-start(bf16[8,64,256]{2,1,0:T(8,128)(2,1)} %get-tuple-element.159), channel_id=1, source_target_pairs={{8,0},{16,8},{24,16},{32,24},{40,32},{48,40},{56,48},{64,56},{72,6... | collective-permute-start | bytes 786440 | tf_op jit(solution)/shard_map/ppermute | solution.py:17
  16.2 10.7 collective-permute-start.3
  18.1 32.9 %collective-permute-start.5 = (bf16[8,64,256]{2,1,0:T(8,128)(2,1)S(1)}, bf16[8,64,256]{2,1,0:T(8,128)(2,1)S(1)}, u32[]{:S(2)}, u32[]{:S(2)}) collective-permute-start(bf16[8,64,256]{2,1,0:T(8,128)(2,1)S(1)} %get-tuple-element.157), channel_id=1, source_target_pairs={{1,0},{2,1},{3,2},{4,3},{5,4},{6,5},{7,6},{9,8},{10,9},{11,10},{12... | collective-permute-start | bytes 786440 | tf_op jit(solution)/shard_map/ppermute | solution.py:17
  19.4 20.8 %collective-permute-start.7 = (bf16[8,64,256]{2,1,0:T(8,128)(2,1)S(1)}, bf16[8,64,256]{2,1,0:T(8,128)(2,1)S(1)}, u32[]{:S(2)}, u32[]{:S(2)}) collective-permute-start(bf16[8,64,256]{2,1,0:T(8,128)(2,1)S(1)} %get-tuple-element.155), channel_id=1, source_target_pairs={{0,8},{8,16},{16,24},{24,32},{32,40},{40,48},{48,56},{56,64},{64,7... | collective-permute-start | bytes 786440 | tf_op jit(solution)/shard_map/ppermute | solution.py:17
  25.2 8.0 collective-permute-start.1
  26.9 33.8 %copy-start = (bf16[1,1,32,64,256]{4,3,2,1,0:T(8,128)(2,1)S(1)}, bf16[1,1,32,64,256]{4,3,2,1,0:T(8,128)(2,1)}, u32[]{:S(2)}) copy-start(bf16[1,1,32,64,256]{4,3,2,1,0:T(8,128)(2,1)} %param.12) | copy-start | bytes 3145732
  26.9 17.2 %collective-permute-start.10 = (bf16[8,64,256]{2,1,0:T(8,128)(2,1)S(1)}, bf16[8,64,256]{2,1,0:T(8,128)(2,1)S(1)}, u32[]{:S(2)}, u32[]{:S(2)}) collective-permute-start(bf16[8,64,256]{2,1,0:T(8,128)(2,1)S(1)} %get-tuple-element.153), channel_id=1, source_target_pairs={{0,8},{8,16},{16,24},{24,32},{32,40},{40,48},{48,56},{56,64},{64,7... | collective-permute-start | bytes 786440 | tf_op jit(solution)/shard_map/ppermute | solution.py:17
  33.2 12.2 %collective-permute-start.4 = (bf16[8,64,256]{2,1,0:T(8,128)(2,1)S(1)}, bf16[8,64,256]{2,1,0:T(8,128)(2,1)S(1)}, u32[]{:S(2)}, u32[]{:S(2)}) collective-permute-start(bf16[8,64,256]{2,1,0:T(8,128)(2,1)S(1)} %collective-permute-done.3), channel_id=1, source_target_pairs={{0,1},{1,2},{2,3},{3,4},{4,5},{5,6},{6,7},{8,9},{9,10},{10,11},{11... | collective-permute-start | bytes 786440 | tf_op jit(solution)/shard_map/ppermute | solution.py:17
  36.9 14.1 %collective-permute-start.6 = (bf16[8,64,256]{2,1,0:T(8,128)(2,1)S(1)}, bf16[8,64,256]{2,1,0:T(8,128)(2,1)S(1)}, u32[]{:S(2)}, u32[]{:S(2)}) collective-permute-start(bf16[8,64,256]{2,1,0:T(8,128)(2,1)S(1)} %get-tuple-element.156), channel_id=1, source_target_pairs={{0,1},{1,2},{2,3},{3,4},{4,5},{5,6},{6,7},{8,9},{9,10},{10,11},{11... | collective-permute-start | bytes 786440 | tf_op jit(solution)/shard_map/ppermute | solution.py:17
  40.2 20.5 %collective-permute-start.9 = (bf16[8,64,256]{2,1,0:T(8,128)(2,1)S(1)}, bf16[8,64,256]{2,1,0:T(8,128)(2,1)S(1)}, u32[]{:S(2)}, u32[]{:S(2)}) collective-permute-start(bf16[8,64,256]{2,1,0:T(8,128)(2,1)S(1)} %get-tuple-element.154), channel_id=1, source_target_pairs={{0,8},{8,16},{16,24},{24,32},{32,40},{40,48},{48,56},{56,64},{64,7... | collective-permute-start | bytes 786440 | tf_op jit(solution)/shard_map/ppermute | solution.py:17
  44.2 10.5 collective-permute-start.8
  45.5 15.2 %collective-permute-start.11 = (bf16[8,64,256]{2,1,0:T(8,128)(2,1)S(1)}, bf16[8,64,256]{2,1,0:T(8,128)(2,1)S(1)}, u32[]{:S(2)}, u32[]{:S(2)}) collective-permute-start(bf16[8,64,256]{2,1,0:T(8,128)(2,1)S(1)} %collective-permute-done.10), channel_id=1, source_target_pairs={{0,1},{1,2},{2,3},{3,4},{4,5},{5,6},{6,7},{8,9},{9,10},{10,11},{11... | collective-permute-start | bytes 786440 | tf_op jit(solution)/shard_map/ppermute | solution.py:17
  833.4 364.8 %all-reduce.9.cloned.1.call-start = ((), (), s32[]{:S(2)}) async-start(), calls=%async_computation.1 | async-start | bytes 14155776 | tf_op jit(solution)/shard_map/psum | solution.py:11
  999.4 3.2 copy-start.6
  999.5 13.2 %copy-start.1 = (bf16[1,1,32,64,256]{4,3,2,1,0:T(8,128)(2,1)S(1)}, bf16[1,1,32,64,256]{4,3,2,1,0:T(8,128)(2,1)}, u32[]{:S(2)}) copy-start(bf16[1,1,32,64,256]{4,3,2,1,0:T(8,128)(2,1)} %param.14) | copy-start | bytes 3145732
  1000.6 9.0 collective-permute-start.12
  1002.7 42.0 %collective-permute-start.14 = (bf16[8,64,256]{2,1,0:T(8,128)(2,1)}, bf16[8,64,256]{2,1,0:T(8,128)(2,1)S(1)}, u32[]{:S(2)}, u32[]{:S(2)}) collective-permute-start(bf16[8,64,256]{2,1,0:T(8,128)(2,1)} %get-tuple-element.149), channel_id=1, source_target_pairs={{0,8},{8,16},{16,24},{24,32},{32,40},{40,48},{48,56},{56,64},{64,7... | collective-permute-start | bytes 786440 | tf_op jit(solution)/shard_map/ppermute | solution.py:17
  1008.1 6.5 copy-start.3
  1008.1 10.7 copy-start.5
  1008.1 13.5 %copy-start.4 = (bf16[8,64,256]{2,1,0:T(8,128)(2,1)S(1)}, bf16[8,64,256]{2,1,0:T(8,128)(2,1)}, u32[]{:S(2)}) copy-start(bf16[8,64,256]{2,1,0:T(8,128)(2,1)} %get-tuple-element.143) | copy-start | bytes 786436
  1008.1 36.6 %copy-start.2 = (bf16[8,64,256]{2,1,0:T(8,128)(2,1)S(1)}, bf16[8,64,256]{2,1,0:T(8,128)(2,1)}, u32[]{:S(2)}) copy-start(bf16[8,64,256]{2,1,0:T(8,128)(2,1)} %get-tuple-element.146) | copy-start | bytes 786436
  1008.2 13.5 %collective-permute-start.15 = (bf16[8,64,256]{2,1,0:T(8,128)(2,1)}, bf16[8,64,256]{2,1,0:T(8,128)(2,1)S(1)}, u32[]{:S(2)}, u32[]{:S(2)}) collective-permute-start(bf16[8,64,256]{2,1,0:T(8,128)(2,1)} %get-tuple-element.148), channel_id=1, source_target_pairs={{1,0},{2,1},{3,2},{4,3},{5,4},{6,5},{7,6},{9,8},{10,9},{11,10},{12... | collective-permute-start | bytes 786440 | tf_op jit(solution)/shard_map/ppermute | solution.py:17
  1009.6 29.1 %collective-permute-start.13 = (bf16[8,64,256]{2,1,0:T(8,128)(2,1)}, bf16[8,64,256]{2,1,0:T(8,128)(2,1)S(1)}, u32[]{:S(2)}, u32[]{:S(2)}) collective-permute-start(bf16[8,64,256]{2,1,0:T(8,128)(2,1)} %collective-permute-done.12), channel_id=1, source_target_pairs={{0,8},{8,16},{16,24},{24,32},{32,40},{40,48},{48,56},{56,64},{64,7... | collective-permute-start | bytes 786440 | tf_op jit(solution)/shard_map/ppermute | solution.py:17
  1014.6 40.5 %collective-permute-start.17 = (bf16[8,64,256]{2,1,0:T(8,128)(2,1)S(1)}, bf16[8,64,256]{2,1,0:T(8,128)(2,1)S(1)}, u32[]{:S(2)}, u32[]{:S(2)}) collective-permute-start(bf16[8,64,256]{2,1,0:T(8,128)(2,1)S(1)} %copy-done.3), channel_id=1, source_target_pairs={{0,1},{1,2},{2,3},{3,4},{4,5},{5,6},{6,7},{8,9},{9,10},{10,11},{11... | collective-permute-start | bytes 786440 | tf_op jit(solution)/shard_map/ppermute | solution.py:17
  1018.9 27.2 %collective-permute-start.19 = (bf16[8,64,256]{2,1,0:T(8,128)(2,1)S(1)}, bf16[8,64,256]{2,1,0:T(8,128)(2,1)S(1)}, u32[]{:S(2)}, u32[]{:S(2)}) collective-permute-start(bf16[8,64,256]{2,1,0:T(8,128)(2,1)S(1)} %copy-done.5), channel_id=1, source_target_pairs={{0,1},{1,2},{2,3},{3,4},{4,5},{5,6},{6,7},{8,9},{9,10},{10,11},{11... | collective-permute-start | bytes 786440 | tf_op jit(solution)/shard_map/ppermute | solution.py:17
  1021.7 26.3 %collective-permute-start.22 = (bf16[8,64,256]{2,1,0:T(8,128)(2,1)S(1)}, bf16[8,64,256]{2,1,0:T(8,128)(2,1)S(1)}, u32[]{:S(2)}, u32[]{:S(2)}) collective-permute-start(bf16[8,64,256]{2,1,0:T(8,128)(2,1)S(1)} %copy-done.4), channel_id=1, source_target_pairs={{1,0},{2,1},{3,2},{4,3},{5,4},{6,5},{7,6},{9,8},{10,9},{11,10},{12... | collective-permute-start | bytes 786440 | tf_op jit(solution)/shard_map/ppermute | solution.py:17
  1038.7 14.4 %collective-permute-start.16 = (bf16[8,64,256]{2,1,0:T(8,128)(2,1)S(1)}, bf16[8,64,256]{2,1,0:T(8,128)(2,1)S(1)}, u32[]{:S(2)}, u32[]{:S(2)}) collective-permute-start(bf16[8,64,256]{2,1,0:T(8,128)(2,1)S(1)} %collective-permute-done.15), channel_id=1, source_target_pairs={{0,8},{8,16},{16,24},{24,32},{32,40},{40,48},{48,56},{56,64},{64,7... | collective-permute-start | bytes 786440 | tf_op jit(solution)/shard_map/ppermute | solution.py:17
  1044.7 10.4 collective-permute-start.18
  1046.1 25.6 %collective-permute-start.21 = (bf16[8,64,256]{2,1,0:T(8,128)(2,1)S(1)}, bf16[8,64,256]{2,1,0:T(8,128)(2,1)S(1)}, u32[]{:S(2)}, u32[]{:S(2)}) collective-permute-start(bf16[8,64,256]{2,1,0:T(8,128)(2,1)S(1)} %get-tuple-element.144), channel_id=1, source_target_pairs={{8,0},{16,8},{24,16},{32,24},{40,32},{48,40},{56,48},{64,56},{72,6... | collective-permute-start | bytes 786440 | tf_op jit(solution)/shard_map/ppermute | solution.py:17
  1048.0 23.6 %collective-permute-start.20 = (bf16[8,64,256]{2,1,0:T(8,128)(2,1)S(1)}, bf16[8,64,256]{2,1,0:T(8,128)(2,1)S(1)}, u32[]{:S(2)}, u32[]{:S(2)}) collective-permute-start(bf16[8,64,256]{2,1,0:T(8,128)(2,1)S(1)} %collective-permute-done.19), channel_id=1, source_target_pairs={{8,0},{16,8},{24,16},{32,24},{40,32},{48,40},{56,48},{64,56},{72,6... | collective-permute-start | bytes 786440 | tf_op jit(solution)/shard_map/ppermute | solution.py:17
  1053.1 26.9 %collective-permute-start.23 = (bf16[8,64,256]{2,1,0:T(8,128)(2,1)S(1)}, bf16[8,64,256]{2,1,0:T(8,128)(2,1)S(1)}, u32[]{:S(2)}, u32[]{:S(2)}) collective-permute-start(bf16[8,64,256]{2,1,0:T(8,128)(2,1)S(1)} %collective-permute-done.22), channel_id=1, source_target_pairs={{8,0},{16,8},{24,16},{32,24},{40,32},{48,40},{56,48},{64,56},{72,6... | collective-permute-start | bytes 786440 | tf_op jit(solution)/shard_map/ppermute | solution.py:17
Sparse Core Ops, SparseCore 0:
  833.5 162.5 all-reduce.6
  998.7 199.4 all-reduce.8
